TPU v7x, 256 devices: a whole 4x4x8 slice. The times are simulated.
256 devices in a mesh: pair: 64 (over y, z, core), red: 4 (over x).
Axes of the slice: x: 4, y: 4, z: 8, core: 2. Of those that a mesh axis runs over, the one named last changes fastest.
Arguments:
- amplitudes: bfloat16 [64, 64, 8192], P('pair', None, 'red'), may hold values from -6 to 6
- integrals: bfloat16 [8192, 8192], P('red'), may hold values from -0.1875 to 0.1875
- occ_irrep: int32 [64], replicated, may hold values from 0 to 7
- vir_irrep: int32 [512], replicated, may hold values from 0 to 7, as said below
- cd_orbitals: int32 [2, 8192], P(None, 'red'), may hold values from 0 to 511
- ab_orbitals: int32 [2, 8192], P(None, 'pair'), may hold values from 0 to 511, as said below
Outputs:
- residual: bfloat16 [64, 64, 8192], P(None, 'red', 'pair')
Inputs may be any that keep to these rules, and one draw needn't show every extreme that they name: `vir_irrep`: D2h irrep labels; each label is held by exactly 64 virtual orbitals. `occ_irrep`: D2h irrep labels. `cd_orbitals`: indices of virtual orbitals. `ab_orbitals`: indices of virtual orbitals; the slab pairs m with m // 128 equal come as 8 blocks of 16 pairs, and ab_irrep[m] = (m % 128) // 16.
All inputs are finite; a program needn't handle non-finite values.
Results may differ from a plain program's by a relative error of at most 0.001.
Values may be sent and summed in bfloat16 or wider, within the bound.
A program may use at most 192 MiB of HBM per device.

v0:
```python
import jax
import jax.numpy as jnp
from jax import lax
from jax.sharding import PartitionSpec as P


def pair_labels(orbitals, vir_irrep):
    labels = lax.broadcasted_iota(jnp.int32, (1, vir_irrep.shape[0]), 1)
    first_label = jnp.sum(jnp.where(orbitals[0][:, None] == labels, vir_irrep[None, :], 0), axis=1)
    second_label = jnp.sum(jnp.where(orbitals[1][:, None] == labels, vir_irrep[None, :], 0), axis=1)
    return jnp.bitwise_xor(first_label, second_label)


def local(amplitudes, integrals, occ_irrep, vir_irrep, cd_orbitals, ab_orbitals):
    own_rows = amplitudes.shape[0]
    occupied = amplitudes.shape[1]
    slab_width = integrals.shape[1]
    first_row = lax.axis_index("pair") * own_rows
    own_irrep = lax.dynamic_slice_in_dim(occ_irrep, first_row, own_rows, 0)
    pair_irrep = jnp.bitwise_xor(own_irrep[:, None], occ_irrep[None, :])
    cd_irrep = pair_labels(cd_orbitals, vir_irrep)
    masked = jnp.where(
        pair_irrep[:, :, None] == cd_irrep[None, None, :],
        amplitudes,
        jnp.zeros((), amplitudes.dtype),
    )
    partial_sums = jnp.dot(
        masked.reshape(own_rows * occupied, masked.shape[2]),
        integrals,
        preferred_element_type=jnp.float32,
    )
    partial_sums = partial_sums.reshape(own_rows, occupied, slab_width)
    moved = lax.all_to_all(partial_sums, "pair", split_axis=2, concat_axis=0, tiled=True)
    summed = lax.psum_scatter(moved, "red", scatter_dimension=1, tiled=True)
    j_rows = summed.shape[1]
    j_irrep = lax.dynamic_slice_in_dim(occ_irrep, lax.axis_index("red") * j_rows, j_rows, 0)
    out_irrep = jnp.bitwise_xor(occ_irrep[:, None], j_irrep[None, :])
    ab_irrep = pair_labels(ab_orbitals, vir_irrep)
    kept = jnp.where(
        out_irrep[:, :, None] == ab_irrep[None, None, :], summed, jnp.zeros((), summed.dtype)
    )
    return kept.astype(jnp.bfloat16)


def solution(mesh):
    in_specs = (P("pair", None, "red"), P("red", None), P(), P(), P(None, "red"), P(None, "pair"))
    out_specs = P(None, "red", "pair")
    return jax.shard_map(local, mesh=mesh, in_specs=in_specs, out_specs=out_specs, check_vma=False)
```

profile of v0, /device:TPU:1, one launch (start us, length us, event | category | flops | bytes accessed | tf_op | source)
XLA Modules:
  0.0 194.9 jit_solution(4072649862004780560)
XLA Ops:
  6.5 0.0 reduce-scatter.2.cloned.1.call-start
  6.5 1.2 dynamic_slice.7
  7.8 1.3 broadcast_xor_fusion.1
  9.1 0.8 fusion.7
  9.9 2.3 %select_reduce_fusion = (s32[2048]{0:T(1024)S(1)}, s32[2048]{0:T(1024)S(1)}) fusion(s32[2048]{0:T(1024)S(1)} %bitcast.23, s32[512]{0:T(512)} %param.9, s32[2048]{0:T(1024)S(1)} %bitcast.22), kind=kLoop, calls=%fused_computation | loop fusion | flops 6287360 | bytes 34816 | tf_op jit(solution)/shard_map/reduce_sum | solution.py:10
  12.2 19.2 %fusion.1 = f32[64,8192]{0,1:T(8,128)} fusion(bf16[2048,8192]{1,0:T(8,128)(2,1)} %param.7, bf16[1,64,2048]{2,1,0:T(8,128)(2,1)} %param.6, s32[2048]{0:T(1024)S(1)} %xor.49, s32[64]{0:T(128)S(1)} %broadcast_xor_fusion.1), kind=kOutput, calls=%fused_computation.7 | convolution fusion | flops 2147745792 | bytes 35922176 | tf_op jit(solution)/shard_map/dot_general | solution.py:27
  31.4 0.5 broadcast.63
  32.0 38.4 %reduce = f32[8192,64]{1,0:T(8,128)} reduce(f32[8192,1,64]{2,1,0:T(1,128)} %bitcast.19, f32[]{:T(128)} %broadcast.63), dimensions={1}, to_apply=%bitcast.16.reduce_sub_computation | reduce | bytes 4194308
  70.4 4.6 %reshape.102 = f32[64,1,8192]{2,1,0:T(1,128)S(1)} reshape(f32[8192,64]{1,0:T(8,128)} %reduce) | data formatting | bytes 4194304
  74.9 64.3 %all_to_all.18 = f32[64,1,8192]{2,1,0:T(1,128)} all-to-all(f32[64,1,8192]{2,1,0:T(1,128)S(1)} %reshape.102), channel_id=1, replica_groups=mesh['pair'=64,'red'=4] {'pair'}, dimensions={0} | all-to-all | bytes 4194304 | tf_op jit(solution)/shard_map/all_to_all | solution.py:33
  139.2 7.5 %reduce.1 = f32[64,8192]{1,0:T(8,128)S(1)} reduce(f32[64,1,8192]{2,1,0:T(1,128)} %all_to_all.18, f32[]{:T(128)} %broadcast.63), dimensions={1}, to_apply=%all_to_all.13.reduce_sub_computation | reduce | bytes 4194308 | tf_op jit(solution)/shard_map/all_to_all | solution.py:33
  146.8 6.6 %reshape.103 = f32[8192,1,64]{2,1,0:T(1,128)} reshape(f32[64,8192]{1,0:T(8,128)S(1)} %reduce.1) | data formatting | bytes 4194304
  153.4 0.0 copy-start.2
  153.4 0.0 copy-start.1
  153.4 3.9 %copy.11 = f32[1,64,64,128]{3,1,2,0:T(8,128)} copy(f32[1,64,64,128]{1,3,2,0:T(8,128)} %bitcast.20) | data formatting | bytes 4194304 | tf_op jit(solution)/shard_map/all_to_all | solution.py:33
  157.2 0.0 reduce-scatter.2.cloned.1.call-update
  157.3 0.0 copy-done.2
  157.3 0.1 dynamic_slice.6
  157.3 0.0 copy-done.1
  157.3 0.0 copy-done
  157.4 0.2 select_reduce_fusion.2
  157.6 0.1 broadcast_xor_fusion
  157.6 28.5 %reduce-scatter.2.cloned.1.call-done = f32[64,16,128]{2,1,0:T(8,128)} async-done(((f32[64,64,128]{2,1,0:T(8,128)}), f32[64,16,128]{2,1,0:T(8,128)}) %reduce-scatter.2.cloned.1.call-update) | async-done | bytes 524304 | tf_op jit(solution)/shard_map/reduce_scatter | solution.py:34
  186.1 1.9 select_convert_fusion
  (4 shorter events, 0.0 us)
Async XLA Ops:
  6.5 179.6 %reduce-scatter.2.cloned.1.call-start = ((), (), s32[]{:S(2)}) async-start(), calls=%async_computation.2 | async-start | bytes 2621440 | tf_op jit(solution)/shard_map/reduce_scatter | solution.py:34
  153.4 3.9 %copy-start.2 = (s32[64]{0:T(128)S(1)}, s32[64]{0:T(128)}, u32[]{:S(2)}) copy-start(s32[64]{0:T(128)} %param.8) | copy-start | bytes 772
  153.4 4.0 %copy-start.1 = (s32[2,128]{1,0:T(2,128)S(1)}, s32[2,128]{1,0:T(2,128)}, u32[]{:S(2)}) copy-start(s32[2,128]{1,0:T(2,128)} %param.11) | copy-start | bytes 3076
  153.4 4.0 %copy-start = (s32[512]{0:T(512)S(1)}, s32[512]{0:T(512)}, u32[]{:S(2)}) copy-start(s32[512]{0:T(512)} %param.9) | copy-start | bytes 6148
Sparse Core Ops, SparseCore 0:
  157.4 28.6 reduce-scatter.1
where the time goes:
time: 195 us
  blocking collectives  64.3 us (33%)
  other arithmetic  51.8 us (27%)
  waiting for transfers between devices  28.5 us (15%)
  matrix products  19.2 us (10%)
  local copies, waits for them, and re-layouts  17.6 us (9%)
  between operations  13.5 us (7%)
    all_to_all x1, blocking collectives, local(): lax.all_to_all(partial_sums, 'pair', split_axis=2, concat_axis=0, tiled=T...  64.3 us
    unnamed x1, other arithmetic  38.4 us
    reduce_scatter x1, waiting for transfers between devices, local(): summed = lax.psum_scatter(moved, 'red', scatter_dimension=1, tiled=True)  28.5 us
    dot_general x1, matrix products, local(): jnp.dot(masked.reshape(own_rows * occupied, masked.shape[2]), integrals,...  19.2 us
    unnamed x9, local copies, waits for them, and re-layouts  11.6 us
    all_to_all x1, other arithmetic, local(): lax.all_to_all(partial_sums, 'pair', split_axis=2, concat_axis=0, tiled=T...  7.54 us
  transfers between devices with their start and end apart: 1, of which 1 were waited for; matrix products, arithmetic and copies ran while one was open for 0% of the time, Pallas kernels for 0%

commit v1 on v0

--- a/solution.py
+++ b/solution.py
@@ -30,7 +30,12 @@
         preferred_element_type=jnp.float32,
     )
     partial_sums = partial_sums.reshape(own_rows, occupied, slab_width)
-    moved = lax.all_to_all(partial_sums, "pair", split_axis=2, concat_axis=0, tiled=True)
+    moved = jnp.concatenate(
+        lax.all_to_all(
+            jnp.stack(jnp.split(partial_sums, lax.axis_size("pair"), axis=2)), "pair", 0, 0
+        ),
+        axis=0,
+    )
     summed = lax.psum_scatter(moved, "red", scatter_dimension=1, tiled=True)
     j_rows = summed.shape[1]
     j_irrep = lax.dynamic_slice_in_dim(occ_irrep, lax.axis_index("red") * j_rows, j_rows, 0)

time: 195 us -> 129 us (0.66)
  other arithmetic: 51.8 us -> 5.84 us
  local copies, waits for them, and re-layouts: 17.6 us -> 3.19 us
  matrix products: 19.2 us -> 13.8 us
    unnamed x1 -> x0, other arithmetic: 38.4 us -> none
    unnamed x9 -> x69, local copies, waits for them, and re-layouts: 11.6 us -> 1.06 us
    all_to_all x1 -> x0, other arithmetic: 7.54 us -> none  [local(): lax.all_to_all(partial_sums, 'pair', split_axis=2, concat_axis=0, tiled=T...]
    dot_general x1, matrix products: 19.2 us -> 13.8 us  [local(): jnp.dot(masked.reshape(own_rows * occupied, masked.shape[2]), integrals,...]
    all_to_all x1 -> x0, local copies, waits for them, and re-layouts: 3.87 us -> none  [local(): lax.all_to_all(partial_sums, 'pair', split_axis=2, concat_axis=0, tiled=T...]
where the time goes in v1:
time: 129 us
  blocking collectives  64.3 us (50%)
  waiting for transfers between devices  27.9 us (22%)
  between operations  13.9 us (11%)
  matrix products  13.8 us (11%)
  other arithmetic  5.84 us (5%)
  local copies, waits for them, and re-layouts  3.19 us (2%)
    all_to_all x1, blocking collectives, local(): lax.all_to_all(jnp.stack(jnp.split(partial_sums, lax.axis_size('pair'), a...  64.3 us
    reduce_scatter x1, waiting for transfers between devices, local(): summed = lax.psum_scatter(moved, 'red', scatter_dimension=1, tiled=True)  27.9 us
    dot_general x1, matrix products, local(): jnp.dot(masked.reshape(own_rows * occupied, masked.shape[2]), integrals,...  13.8 us
  transfers between devices with their start and end apart: 1, of which 1 were waited for; matrix products, arithmetic and copies ran while one was open for 0% of the time, Pallas kernels for 0%

profile of v1, /device:TPU:1, one launch (start us, length us, event | category | flops | bytes accessed | tf_op | source)
XLA Modules:
  0.0 129.0 jit_solution(4237532948766741359)
XLA Ops:
  6.5 0.0 reduce-scatter.2.cloned.1.call-start
  6.5 1.2 dynamic_slice.7
  7.8 1.3 %broadcast_xor_fusion.1 = s32[64]{0:T(128)S(1)} fusion(s32[64]{0:T(128)} %param.8, s32[]{:T(128)} %bitcast.2), kind=kLoop, calls=%fused_computation.146 | loop fusion | flops 64 | bytes 516 | tf_op jit(solution)/shard_map/xor | solution.py:20
  9.1 0.8 fusion.6
  9.9 2.3 %select_reduce_fusion = (s32[2048]{0:T(1024)S(1)}, s32[2048]{0:T(1024)S(1)}) fusion(s32[2048]{0:T(1024)S(1)} %bitcast.272, s32[512]{0:T(512)} %param.9, s32[2048]{0:T(1024)S(1)} %bitcast.271), kind=kLoop, calls=%fused_computation.1 | loop fusion | flops 6287360 | bytes 34816 | tf_op jit(solution)/shard_map/reduce_sum | solution.py:10
  12.2 13.8 %convolution_bitcast_fusion = f32[1,64,8192]{2,1,0:T(8,128)S(1)} fusion(bf16[2048,8192]{1,0:T(8,128)(2,1)} %param.7, bf16[1,64,2048]{2,1,0:T(8,128)(2,1)} %param.6, s32[2048]{0:T(1024)S(1)} %xor.49, s32[64]{0:T(128)S(1)} %broadcast_xor_fusion.1), kind=kOutput, calls=%fused_computation | convolution fusion | flops 2147745792 | bytes 35922176 | tf_op jit(solution)/shard_map/dot_general | solution.py:27
  26.9 64.3 %all_to_all.5 = f32[64,1,64,128]{3,2,1,0:T(8,128)} all-to-all(f32[64,1,64,128]{3,2,1,0:T(8,128)S(1)} %constant_dynamic-update-slice_fusion), channel_id=1, replica_groups=mesh['pair'=64,'red'=4] {'pair'}, dimensions={0} | all-to-all | bytes 4194304 | tf_op jit(solution)/shard_map/all_to_all | solution.py:34
  91.3 0.0 copy-start.2
  91.3 0.0 copy-start.1
  91.3 0.0 copy-start
  91.3 0.0 reduce-scatter.2.cloned.1.call-update
  91.3 0.6 copy-done.2
  91.9 0.1 dynamic_slice.6
  92.0 0.0 copy-done.1
  92.0 0.0 copy-done
  92.0 0.2 select_reduce_fusion.2
  92.2 0.1 broadcast_xor_fusion
  92.3 27.9 %reduce-scatter.2.cloned.1.call-done = f32[64,16,128]{2,1,0:T(8,128)} async-done(((f32[64,64,128]{2,1,0:T(8,128)}), f32[64,16,128]{2,1,0:T(8,128)}) %reduce-scatter.2.cloned.1.call-update) | async-done | bytes 524304 | tf_op jit(solution)/shard_map/reduce_scatter | solution.py:39
  120.2 1.9 %select_convert_fusion = bf16[64,16,128]{2,1,0:T(8,128)(2,1)} fusion(f32[64,16,128]{2,1,0:T(8,128)} %reduce-scatter.2.cloned.1.call-done, s32[128]{0:T(128)S(1)} %xor.45, s32[64,16]{1,0:T(8,128)S(1)} %broadcast_xor_fusion), kind=kLoop, calls=%fused_computation.5 | loop fusion | flops 262144 | bytes 791040 | tf_op jit(solution)/shard_map/convert_element_type | solution.py:47
  (67 shorter events, 0.5 us)
Async XLA Ops:
  6.5 113.6 %reduce-scatter.2.cloned.1.call-start = ((), (), s32[]{:S(2)}) async-start(), calls=%async_computation.2 | async-start | bytes 2621440 | tf_op jit(solution)/shard_map/reduce_scatter | solution.py:39
  91.3 0.7 copy-start.2
  91.3 0.7 copy-start.1
  91.3 0.7 copy-start
Sparse Core Ops, SparseCore 0:
  91.4 28.7 reduce-scatter.1
